TPU v7x, 32 devices: a whole 2x2x4 slice. The times are simulated.
32 devices in a mesh: dp: 8 (over y, x, core), mp: 4 (over z).
Axes of the slice: x: 2, y: 2, z: 4, core: 2. Of those that a mesh axis runs over, the one named last changes fastest.
Arguments:
- tokens: bfloat16 [32768, 512], P(('dp', 'mp')), may hold values from -6 to 6
- qkv_weight: bfloat16 [512, 1536], replicated, may hold values from -0.25 to 0.25
- out_weight: bfloat16 [512, 512], replicated, may hold values from -2 to 2
- norm1_gain: float32 [512], replicated, may hold values from 0.1 to 1.9
- norm1_shift: float32 [512], replicated, may hold values from -3 to 3
- norm2_gain: float32 [512], replicated, may hold values from 0.1 to 1.9
- norm2_shift: float32 [512], replicated, may hold values from -3 to 3
- up_weight: bfloat16 [512, 2048], P(None, 'mp'), may hold values from -0.25 to 0.25
- up_bias: bfloat16 [2048], P('mp'), may hold values from -3 to 3
- down_weight: bfloat16 [2048, 512], P('mp'), may hold values from -0.125 to 0.125
- down_bias: float32 [512], replicated, may hold values from -3 to 3
- lengths: int32 [17], replicated, may hold values from 512 to 16384, as said below
- cotangent: bfloat16 [32768, 512], P(('dp', 'mp')), may hold values from -6 to 6
Outputs:
- output: bfloat16 [32768, 512], P(('dp', 'mp'))
- input_grad: bfloat16 [32768, 512], P(('dp', 'mp'))
- qkv_grad: float32 [512, 1536], replicated
- out_grad: float32 [512, 512], replicated
- norm1_gain_grad: float32 [512], replicated
- norm1_shift_grad: float32 [512], replicated
- norm2_gain_grad: float32 [512], replicated
- norm2_shift_grad: float32 [512], replicated
- up_grad: float32 [512, 2048], P(None, 'mp')
- up_bias_grad: float32 [2048], P('mp')
- down_grad: float32 [2048, 512], P('mp')
- down_bias_grad: float32 [512], replicated
Inputs may be any that keep to these rules, and one draw needn't show every extreme that they name: The 17 lengths add up to 32768; 1 of them equal 16384, and the others lie between 512 and 1536, both ends reached.
All inputs are finite; a program needn't handle non-finite values.
Results may differ from a plain program's by a relative error of at most 0.012.
Values may be sent and summed in bfloat16 or wider, within the bound.
No kernel may reach another device: no remote copies, remote signals or barrier semaphores. Data moves between devices by JAX's collectives and lax.ppermute only.
A program may use at most 192 MiB of HBM per device.

v0:
```python
import jax
import jax.numpy as jnp
from jax import lax
from jax.sharding import PartitionSpec as P

HEADS = 8
HEAD_DIM = 64
BLK = 512
NORM_EPS = 1e-05
SCORE_EPS = 1e-06
EXACT_MODE = lax.Precision.HIGHEST


def carried_in(array, axis, combine, identity):
    peers, position = (lax.axis_size(axis), lax.axis_index(axis))
    everything = jax.tree.map(
        lambda part, kind: lax.all_gather(part.astype(kind), axis),
        array,
        (jnp.bfloat16, jnp.bfloat16, jnp.bfloat16),
    )
    start = jax.tree.map(
        lambda part, zero: jnp.broadcast_to(jnp.asarray(zero, part.dtype), part.shape),
        array,
        identity,
    )

    def lap(k, before):
        reached = k < position
        new = combine(
            before, jax.tree.map(lambda part, own: part[k].astype(own.dtype), everything, array)
        )
        return jax.tree.map(lambda a, b: jnp.where(reached, a, b), new, before)

    return lax.fori_loop(0, peers, lap, start)


def carried_in_2(array, axis, join, neutral):
    count = lax.axis_size(axis)
    place = lax.axis_index(axis)
    ahead = count - 1 - place
    gathered = jax.tree.map(
        lambda a, kind: lax.all_gather(a.astype(kind), axis),
        array,
        jax.tree.map(lambda a: jnp.bfloat16 if a.dtype == jnp.float32 else a.dtype, array),
    )
    state = jax.tree.map(lambda a, e: jnp.zeros_like(a) + jnp.asarray(e, a.dtype), array, neutral)

    def one(lap, state):
        source = count - 1 - lap
        return join(
            state,
            jax.tree.map(
                lambda a, own: lax.dynamic_index_in_dim(a, source, 0, False).astype(own.dtype),
                gathered,
                array,
            ),
        )

    return lax.fori_loop(0, ahead, one, state)


def normalize(rows, gain, shift):
    centred = rows - jnp.mean(rows, axis=-1, keepdims=True)
    inv_std = lax.rsqrt(jnp.mean(centred * centred, axis=-1, keepdims=True) + NORM_EPS)
    scaled = centred * inv_std
    return (scaled * gain + shift, scaled, inv_std)


def normalize_back(upstream, scaled, inv_std, gain):
    weighted = upstream * gain
    centred = weighted - jnp.mean(weighted, axis=-1, keepdims=True)
    inner = centred - scaled * jnp.mean(weighted * scaled, axis=-1, keepdims=True)
    return (inner * inv_std, jnp.sum(upstream * scaled, axis=0), jnp.sum(upstream, axis=0))


def feature_map(values):
    return jax.nn.elu(values) + 1.0


def feature_slope(values):
    return jnp.where(values > 0, 1.0, jnp.exp(jnp.minimum(values, 0.0)))


def gelu_slope(values):
    return (
        0.5 * (1.0 + lax.erf(values * 0.7071067811865476))
        + values * jnp.exp(-0.5 * values * values) * 0.3989422804014327
    )


def segment_rows(lengths, first, count):
    ends = jnp.cumsum(lengths)
    starts = ends - lengths
    places = first + jnp.arange(count, dtype=jnp.int32)
    segment = jnp.sum((ends[None, :] <= places[:, None]).astype(jnp.int32), axis=1)
    opening = jnp.sum((starts[None, :] == places[:, None]).astype(jnp.int32), axis=1)
    return (segment, opening)


def block_masks(segment, opening, start):
    block_seg = lax.dynamic_slice_in_dim(segment, start, BLK)
    first_open = lax.dynamic_slice_in_dim(opening, start, 1)[0]
    carried = ((block_seg == block_seg[0]) & (first_open == 0)).astype(jnp.float32)
    ending = (block_seg == block_seg[-1]).astype(jnp.float32)
    places = jnp.arange(BLK)
    allowed = (
        (places[None, :] <= places[:, None]) & (block_seg[None, :] == block_seg[:, None])
    ).astype(jnp.float32)
    return (carried, ending, allowed)


def join_states(earlier, later):
    keep = 1.0 - later[2]
    return (
        later[0] + keep * earlier[0],
        later[1] + keep * earlier[1],
        jnp.maximum(earlier[2], later[2]),
    )


def local(
    tokens,
    qkv_weight,
    out_weight,
    norm1_gain,
    norm1_shift,
    norm2_gain,
    norm2_shift,
    up_weight,
    up_bias,
    down_weight,
    down_bias,
    lengths,
    cotangent,
):
    rows = tokens.shape[0]
    width = tokens.shape[1]
    span = rows * lax.axis_size("mp")
    blocks = span // BLK
    group_first = lax.axis_index("dp") * span
    own_start = lax.axis_index("mp") * rows
    segment, opening = segment_rows(lengths, group_first, span)
    continuing = ((segment == segment[0]) & (opening[0] == 0)).astype(jnp.float32)
    reset = 1.0 - continuing[-1]
    inputs = tokens.astype(jnp.float32)
    normed_one, scaled_one, inv_one = normalize(inputs, norm1_gain, norm1_shift)
    normed_low = normed_one.astype(jnp.bfloat16)
    group_rows = lax.all_gather(normed_low, "mp", axis=0, tiled=True)

    def features(start):
        rows_in = lax.dynamic_slice_in_dim(group_rows, start, BLK)
        projected = jnp.dot(rows_in, qkv_weight, preferred_element_type=jnp.float32)
        query = projected[:, :width].reshape(BLK, HEADS, HEAD_DIM)
        keys = projected[:, width : 2 * width].reshape(BLK, HEADS, HEAD_DIM)
        values = projected[:, 2 * width :].reshape(BLK, HEADS, HEAD_DIM)
        return (query, keys, values)

    def forward_block(carry, index):
        state, total = carry
        start = index * BLK
        query, keys, values = features(start)
        query_low = feature_map(query).astype(jnp.bfloat16)
        key_low = feature_map(keys).astype(jnp.bfloat16)
        value_low = values.astype(jnp.bfloat16)
        carried, ending, allowed = block_masks(segment, opening, start)
        scores = (
            jnp.einsum("ihd,jhd->hij", query_low, key_low, preferred_element_type=jnp.float32)
            * allowed[None]
        )
        query_wide = query_low.astype(jnp.float32)
        numerator = jnp.einsum(
            "hij,jhd->ihd",
            scores.astype(jnp.bfloat16),
            value_low,
            preferred_element_type=jnp.float32,
        )
        numerator = numerator + carried[:, None, None] * jnp.einsum(
            "ihd,hde->ihe", query_wide, state, precision=EXACT_MODE
        )
        denominator = (
            jnp.sum(scores, axis=-1).T
            + carried[:, None] * jnp.einsum("ihd,hd->ih", query_wide, total, precision=EXACT_MODE)
            + SCORE_EPS
        )
        keep = carried[-1]
        key_end = key_low * ending.astype(jnp.bfloat16)[:, None, None]
        new_state = keep * state + jnp.einsum(
            "jhd,jhe->hde", key_end, value_low, preferred_element_type=jnp.float32
        )
        new_total = keep * total + jnp.sum(key_end.astype(jnp.float32), axis=0)
        return ((new_state, new_total), (numerator, denominator, query_low, state, total))

    zero_state = jnp.zeros((HEADS, HEAD_DIM, HEAD_DIM), jnp.float32)
    zero_total = jnp.zeros((HEADS, HEAD_DIM), jnp.float32)
    nothing = jnp.zeros((), jnp.float32)
    (state_end, total_end), kept = lax.scan(
        forward_block, (zero_state, zero_total), jnp.arange(blocks, dtype=jnp.int32)
    )
    numerator = kept[0].reshape(span, HEADS, HEAD_DIM)
    denominator = kept[1].reshape(span, HEADS)
    query_all = kept[2].reshape(span, HEADS, HEAD_DIM)
    block_states = kept[3]
    block_totals = kept[4]
    state_in, total_in, _ = carried_in(
        (state_end, total_end, reset), "dp", join_states, (zero_state, zero_total, nothing)
    )
    query_wide = query_all.astype(jnp.float32)
    numerator = numerator + continuing[:, None, None] * jnp.einsum(
        "ihd,hde->ihe", query_wide, state_in, precision=EXACT_MODE
    )
    denominator = denominator + continuing[:, None] * jnp.einsum(
        "ihd,hd->ih", query_wide, total_in, precision=EXACT_MODE
    )
    context = numerator / denominator[:, :, None]
    context_low = lax.dynamic_slice_in_dim(context.reshape(span, width), own_start, rows).astype(
        jnp.bfloat16
    )
    attended = jnp.dot(context_low, out_weight, preferred_element_type=jnp.float32)
    residual = inputs + attended
    normed_two, scaled_two, inv_two = normalize(residual, norm2_gain, norm2_shift)
    second_low = normed_two.astype(jnp.bfloat16)
    cotangent_wide = cotangent.astype(jnp.float32)
    group_second = lax.all_gather(second_low, "mp", axis=0, tiled=True)
    hidden_in = jnp.dot(group_second, up_weight, preferred_element_type=jnp.float32) + up_bias
    hidden_low = jax.nn.gelu(hidden_in, approximate=False).astype(jnp.bfloat16)
    ffn_out = lax.psum_scatter(
        jnp.dot(hidden_low, down_weight, preferred_element_type=jnp.float32).astype(jnp.bfloat16),
        "mp",
        scatter_dimension=0,
        tiled=True,
    ).astype(jnp.float32)
    group_cotangent = lax.all_gather(cotangent, "mp", axis=0, tiled=True)
    grad_down = jnp.einsum(
        "tf,td->fd", hidden_low, group_cotangent, preferred_element_type=jnp.float32
    )
    grad_hidden = jnp.einsum(
        "td,fd->tf", group_cotangent, down_weight, preferred_element_type=jnp.float32
    )
    hidden_grad = (grad_hidden * gelu_slope(hidden_in)).astype(jnp.bfloat16)
    grad_up_bias = jnp.sum(hidden_grad.astype(jnp.float32), axis=0)
    grad_up = jnp.einsum("td,tf->df", group_second, hidden_grad, preferred_element_type=jnp.float32)
    grad_second = lax.psum_scatter(
        jnp.einsum("tf,df->td", hidden_grad, up_weight, preferred_element_type=jnp.float32).astype(
            jnp.bfloat16
        ),
        "mp",
        scatter_dimension=0,
        tiled=True,
    ).astype(jnp.float32)
    grad_up, grad_up_bias, grad_down = lax.psum((grad_up, grad_up_bias, grad_down), "dp")
    output = (residual + ffn_out + down_bias).astype(jnp.bfloat16)
    grad_second_in, grad_gain_two, grad_shift_two = normalize_back(
        grad_second, scaled_two, inv_two, norm2_gain
    )
    grad_residual = cotangent_wide + grad_second_in
    grad_attended = grad_residual.astype(jnp.bfloat16)
    grad_out = jnp.einsum(
        "ti,to->io", context_low, grad_attended, preferred_element_type=jnp.float32
    )
    grad_context_own = jnp.einsum(
        "to,io->ti", grad_attended, out_weight, preferred_element_type=jnp.float32
    ).astype(jnp.bfloat16)
    grad_context = (
        lax.all_gather(grad_context_own, "mp", axis=0, tiled=True)
        .astype(jnp.float32)
        .reshape(span, HEADS, HEAD_DIM)
    )
    grad_numer = (grad_context / denominator[:, :, None]).astype(jnp.bfloat16)
    grad_denom = -jnp.sum(grad_context * context, axis=-1) / denominator
    local_state = jnp.einsum(
        "ihd,ihe->hde",
        query_all * continuing.astype(jnp.bfloat16)[:, None, None],
        grad_numer,
        preferred_element_type=jnp.float32,
    )
    local_total = jnp.einsum(
        "ih,ihd->hd", continuing[:, None] * grad_denom, query_wide, precision=EXACT_MODE
    )
    state_back, total_back, _ = carried_in_2(
        (local_state, local_total, reset), "dp", join_states, (zero_state, zero_total, nothing)
    )
    prior = jnp.concatenate([jnp.ones((1,), jnp.float32), continuing[BLK - 1 :: BLK][:-1]])
    true_states = block_states + prior[:, None, None, None] * state_in[None]
    true_totals = block_totals + prior[:, None, None] * total_in[None]

    def back_block(carry, index):
        state_grad, total_grad = carry
        start = index * BLK
        query, keys, values = features(start)
        query_low = feature_map(query).astype(jnp.bfloat16)
        key_low = feature_map(keys).astype(jnp.bfloat16)
        value_low = values.astype(jnp.bfloat16)
        carried, ending, allowed = block_masks(segment, opening, start)
        state = true_states[index]
        total = true_totals[index]
        numer_grad = lax.dynamic_slice_in_dim(grad_numer, start, BLK)
        denom_grad = lax.dynamic_slice_in_dim(grad_denom, start, BLK)
        scores = (
            jnp.einsum("ihd,jhd->hij", query_low, key_low, preferred_element_type=jnp.float32)
            * allowed[None]
        )
        weights = scores.astype(jnp.bfloat16)
        weight_grad = (
            jnp.einsum("ihe,jhe->hij", numer_grad, value_low, preferred_element_type=jnp.float32)
            + denom_grad.T[:, :, None]
        )
        score_grad = weight_grad.astype(jnp.bfloat16) * allowed.astype(jnp.bfloat16)[None]
        query_wide_blk = query_low.astype(jnp.float32)
        numer_wide = numer_grad.astype(jnp.float32)
        query_grad = jnp.einsum(
            "hij,jhd->ihd", score_grad, key_low, preferred_element_type=jnp.float32
        )
        query_grad = query_grad + carried[:, None, None] * (
            jnp.einsum("ihe,hde->ihd", numer_wide, state, precision=EXACT_MODE)
            + denom_grad[:, :, None] * total[None]
        )
        key_grad = jnp.einsum(
            "hij,ihd->jhd", score_grad, query_low, preferred_element_type=jnp.float32
        )
        key_grad = key_grad + ending[:, None, None] * (
            jnp.einsum(
                "jhe,hde->jhd", value_low.astype(jnp.float32), state_grad, precision=EXACT_MODE
            )
            + total_grad[None]
        )
        value_grad = jnp.einsum(
            "hij,ihd->jhd", weights, numer_grad, preferred_element_type=jnp.float32
        )
        value_grad = value_grad + ending[:, None, None] * jnp.einsum(
            "jhd,hde->jhe", key_low.astype(jnp.float32), state_grad, precision=EXACT_MODE
        )
        keep = carried[-1]
        prev_state = keep * state_grad + jnp.einsum(
            "ihd,ihe->hde",
            query_low * carried.astype(jnp.bfloat16)[:, None, None],
            numer_grad,
            preferred_element_type=jnp.float32,
        )
        prev_total = keep * total_grad + jnp.einsum(
            "ih,ihd->hd", carried[:, None] * denom_grad, query_wide_blk, precision=EXACT_MODE
        )
        joined = jnp.concatenate(
            [
                (query_grad * feature_slope(query)).reshape(BLK, width),
                (key_grad * feature_slope(keys)).reshape(BLK, width),
                value_grad.reshape(BLK, width),
            ],
            axis=1,
        )
        return ((prev_state, prev_total), joined.astype(jnp.bfloat16))

    _, grad_blocks = lax.scan(
        back_block, (state_back, total_back), jnp.arange(blocks, dtype=jnp.int32), reverse=True
    )
    grad_projected = lax.dynamic_slice_in_dim(grad_blocks.reshape(span, 3 * width), own_start, rows)
    grad_qkv = jnp.einsum(
        "td,tk->dk", normed_low, grad_projected, preferred_element_type=jnp.float32
    )
    grad_first = jnp.einsum(
        "tk,dk->td", grad_projected, qkv_weight, preferred_element_type=jnp.float32
    )
    grad_first_in, grad_gain_one, grad_shift_one = normalize_back(
        grad_first, scaled_one, inv_one, norm1_gain
    )
    input_grad = (grad_residual + grad_first_in).astype(jnp.bfloat16)
    grad_down_bias = jnp.sum(cotangent_wide, axis=0)
    summed = lax.psum(
        (
            grad_qkv,
            grad_out,
            grad_gain_one,
            grad_shift_one,
            grad_gain_two,
            grad_shift_two,
            grad_down_bias,
        ),
        ("dp", "mp"),
    )
    return (
        output,
        input_grad,
        summed[0],
        summed[1],
        summed[2],
        summed[3],
        summed[4],
        summed[5],
        grad_up,
        grad_up_bias,
        grad_down,
        summed[6],
    )


def solution(mesh):
    in_specs = (
        P(("dp", "mp"), None),
        P(),
        P(),
        P(),
        P(),
        P(),
        P(),
        P(None, "mp"),
        P("mp"),
        P("mp", None),
        P(),
        P(),
        P(("dp", "mp"), None),
    )
    out_specs = (
        P(("dp", "mp"), None),
        P(("dp", "mp"), None),
        P(),
        P(),
        P(),
        P(),
        P(),
        P(),
        P(None, "mp"),
        P("mp"),
        P("mp", None),
        P(),
    )
    return jax.shard_map(local, mesh=mesh, in_specs=in_specs, out_specs=out_specs, check_vma=False)
```

profile of v0, /device:TPU:0, one launch (start us, length us, event | category | flops | bytes accessed | tf_op | source)
XLA Modules:
  0.0 1671.2 jit_solution(14207868749321259398)
XLA Ops:
  17.8 15.2 all-reduce
  33.1 62.3 %all-gather.9.cloned.1.call-done = bf16[4096,512]{0,1:T(8,128)(2,1)} async-done(((bf16[1024,512]{0,1:T(8,128)(2,1)}), bf16[4096,512]{0,1:T(8,128)(2,1)}) %all-gather.9.cloned.1.call-update) | async-done | bytes 4194320 | tf_op jit(solution)/shard_map/all_gather | solution.py:148
  101.9 482.7 %while.75 = (s32[]{:T(128)}, f32[8,64,64]{2,1,0:T(8,128)S(1)}, f32[8,64]{1,0:T(8,128)S(1)}, f32[8,512,8,64]{1,0,3,2:T(8,128)}, f32[8,512,8]{1,2,0:T(8,128)}, /*i...) while((s32[]{:T(128)}, f32[8,64,64]{2,1,0:T(8,128)S(1)}, ...), condition=%wide.region_8.9_spmd.clone, body=%wide.region_5.8_spmd.clone.sunk | while | flops 1599254528 | bytes 64349520 | solution.py:196
  133.0 21.8 %dynamic_update_slice.51 = f32[8,512,8,64]{1,0,3,2:T(8,128)} dynamic-update-slice(f32[8,512,8,64]{1,0,3,2:T(8,128)} %get-tuple-element.1293, f32[1,512,8,64]{1,0,3,2:T(1,128)S(1)} %copy.224, s32[]{:T(128)} %get-tuple-element.1290, s32[]{:T(128)} %constant.253.clone.1..sunk.2, s32[]{:T(128)} %constant.253.clone.1..sunk.2, s32[]{:T(128)} %constant.253.clone.1..sunk.2) | dynamic-update-slice | bytes 2097156 | tf_op jit(solution)/shard_map/while/body/jit(dynamic_update_index_in_dim)/dynamic_update_slice | solution.py:196
  193.4 21.8 %dynamic_update_slice.51 = f32[8,512,8,64]{1,0,3,2:T(8,128)} dynamic-update-slice(f32[8,512,8,64]{1,0,3,2:T(8,128)} %get-tuple-element.1293, f32[1,512,8,64]{1,0,3,2:T(1,128)S(1)} %copy.224, s32[]{:T(128)} %get-tuple-element.1290, s32[]{:T(128)} %constant.253.clone.1..sunk.2, s32[]{:T(128)} %constant.253.clone.1..sunk.2, s32[]{:T(128)} %constant.253.clone.1..sunk.2) | dynamic-update-slice | bytes 2097156 | tf_op jit(solution)/shard_map/while/body/jit(dynamic_update_index_in_dim)/dynamic_update_slice | solution.py:196
  253.7 21.8 %dynamic_update_slice.51 = f32[8,512,8,64]{1,0,3,2:T(8,128)} dynamic-update-slice(f32[8,512,8,64]{1,0,3,2:T(8,128)} %get-tuple-element.1293, f32[1,512,8,64]{1,0,3,2:T(1,128)S(1)} %copy.224, s32[]{:T(128)} %get-tuple-element.1290, s32[]{:T(128)} %constant.253.clone.1..sunk.2, s32[]{:T(128)} %constant.253.clone.1..sunk.2, s32[]{:T(128)} %constant.253.clone.1..sunk.2) | dynamic-update-slice | bytes 2097156 | tf_op jit(solution)/shard_map/while/body/jit(dynamic_update_index_in_dim)/dynamic_update_slice | solution.py:196
  314.0 21.8 %dynamic_update_slice.51 = f32[8,512,8,64]{1,0,3,2:T(8,128)} dynamic-update-slice(f32[8,512,8,64]{1,0,3,2:T(8,128)} %get-tuple-element.1293, f32[1,512,8,64]{1,0,3,2:T(1,128)S(1)} %copy.224, s32[]{:T(128)} %get-tuple-element.1290, s32[]{:T(128)} %constant.253.clone.1..sunk.2, s32[]{:T(128)} %constant.253.clone.1..sunk.2, s32[]{:T(128)} %constant.253.clone.1..sunk.2) | dynamic-update-slice | bytes 2097156 | tf_op jit(solution)/shard_map/while/body/jit(dynamic_update_index_in_dim)/dynamic_update_slice | solution.py:196
  374.4 21.8 %dynamic_update_slice.51 = f32[8,512,8,64]{1,0,3,2:T(8,128)} dynamic-update-slice(f32[8,512,8,64]{1,0,3,2:T(8,128)} %get-tuple-element.1293, f32[1,512,8,64]{1,0,3,2:T(1,128)S(1)} %copy.224, s32[]{:T(128)} %get-tuple-element.1290, s32[]{:T(128)} %constant.253.clone.1..sunk.2, s32[]{:T(128)} %constant.253.clone.1..sunk.2, s32[]{:T(128)} %constant.253.clone.1..sunk.2) | dynamic-update-slice | bytes 2097156 | tf_op jit(solution)/shard_map/while/body/jit(dynamic_update_index_in_dim)/dynamic_update_slice | solution.py:196
  434.7 21.8 %dynamic_update_slice.51 = f32[8,512,8,64]{1,0,3,2:T(8,128)} dynamic-update-slice(f32[8,512,8,64]{1,0,3,2:T(8,128)} %get-tuple-element.1293, f32[1,512,8,64]{1,0,3,2:T(1,128)S(1)} %copy.224, s32[]{:T(128)} %get-tuple-element.1290, s32[]{:T(128)} %constant.253.clone.1..sunk.2, s32[]{:T(128)} %constant.253.clone.1..sunk.2, s32[]{:T(128)} %constant.253.clone.1..sunk.2) | dynamic-update-slice | bytes 2097156 | tf_op jit(solution)/shard_map/while/body/jit(dynamic_update_index_in_dim)/dynamic_update_slice | solution.py:196
  495.0 21.8 %dynamic_update_slice.51 = f32[8,512,8,64]{1,0,3,2:T(8,128)} dynamic-update-slice(f32[8,512,8,64]{1,0,3,2:T(8,128)} %get-tuple-element.1293, f32[1,512,8,64]{1,0,3,2:T(1,128)S(1)} %copy.224, s32[]{:T(128)} %get-tuple-element.1290, s32[]{:T(128)} %constant.253.clone.1..sunk.2, s32[]{:T(128)} %constant.253.clone.1..sunk.2, s32[]{:T(128)} %constant.253.clone.1..sunk.2) | dynamic-update-slice | bytes 2097156 | tf_op jit(solution)/shard_map/while/body/jit(dynamic_update_index_in_dim)/dynamic_update_slice | solution.py:196
  555.3 21.8 %dynamic_update_slice.51 = f32[8,512,8,64]{1,0,3,2:T(8,128)} dynamic-update-slice(f32[8,512,8,64]{1,0,3,2:T(8,128)} %get-tuple-element.1293, f32[1,512,8,64]{1,0,3,2:T(1,128)S(1)} %copy.224, s32[]{:T(128)} %get-tuple-element.1290, s32[]{:T(128)} %constant.253.clone.1..sunk.2, s32[]{:T(128)} %constant.253.clone.1..sunk.2, s32[]{:T(128)} %constant.253.clone.1..sunk.2) | dynamic-update-slice | bytes 2097156 | tf_op jit(solution)/shard_map/while/body/jit(dynamic_update_index_in_dim)/dynamic_update_slice | solution.py:196
  584.6 10.9 all-gather
  604.6 22.9 %while.76 = (s32[]{:T(128)}, f32[8,64,64]{2,1,0:T(8,128)}, f32[8,64]{1,0:T(8,128)S(1)}, s32[]{:T(128)}, bf16[8,8,64,64]{3,2,1,0:T(8,128)(2,1)S(1)}, /*index=5*/b...) while((s32[]{:T(128)}, f32[8,64,64]{2,1,0:T(8,128)}, ...), condition=%wide.region_10.11_spmd.clone, body=%wide.region_9.10_spmd.clone.sunk | while | flops 166405 | bytes 332957 | solution.py:34
  660.8 76.4 %all-gather.11.cloned.1.call-done = bf16[4096,512]{0,1:T(8,128)(2,1)} async-done(((bf16[1024,512]{0,1:T(8,128)(2,1)}), bf16[4096,512]{0,1:T(8,128)(2,1)}) %all-gather.11.cloned.1.call-update) | async-done | bytes 4194320 | tf_op jit(solution)/shard_map/all_gather | solution.py:223
  737.2 22.8 %fusion.89 = (bf16[4096,512]{1,0:T(8,128)(2,1)}, f32[4096,512]{1,0:T(8,128)}) fusion(f32[512]{0:T(512)} %convert_element_type.335, bf16[4096,512]{0,1:T(8,128)(2,1)} %all-gather.11.cloned.1.call-done, bf16[512,512]{1,0:T(8,128)(2,1)S(1)} %copy-done), kind=kOutput, calls=%fused_computation.135 | convolution fusion | flops 2285895680 | bytes 17303552 | tf_op jit(solution)/shard_map/dot_general | solution.py:224
  760.0 58.0 %all-gather.13.cloned.1.call-done = bf16[4096,512]{1,0:T(8,128)(2,1)} async-done(((bf16[1024,512]{1,0:T(8,128)(2,1)}), bf16[4096,512]{1,0:T(8,128)(2,1)}) %all-gather.13.cloned.1.call-update) | async-done | bytes 4194320 | tf_op jit(solution)/shard_map/all_gather | solution.py:232
  853.7 55.1 %reduce-scatter.5.cloned.1.call-done = bf16[1024,512]{0,1:T(8,128)(2,1)} async-done(((bf16[4096,512]{0,1:T(8,128)(2,1)}), bf16[1024,512]{0,1:T(8,128)(2,1)}) %reduce-scatter.5.cloned.1.call-update) | async-done | bytes 1048592 | tf_op jit(solution)/shard_map/reduce_scatter | solution.py:242
  911.5 76.8 %reduce-scatter.3.cloned.1.call-done = bf16[1024,512]{0,1:T(8,128)(2,1)} async-done(((bf16[4096,512]{0,1:T(8,128)(2,1)}), bf16[1024,512]{0,1:T(8,128)(2,1)}) %reduce-scatter.3.cloned.1.call-update) | async-done | bytes 1048592 | tf_op jit(solution)/shard_map/reduce_scatter | solution.py:226
  1011.1 66.3 %all-gather.15.cloned.1.call-done = bf16[4096,512]{1,0:T(8,128)(2,1)} async-done(((bf16[1024,512]{1,0:T(8,128)(2,1)}), bf16[4096,512]{1,0:T(8,128)(2,1)}) %all-gather.15.cloned.1.call-update) | async-done | bytes 4194320 | tf_op jit(solution)/shard_map/all_gather | solution.py:264
  1111.1 13.4 all-gather.2
  1139.8 371.0 %while.74 = (s32[]{:T(128)}, f32[8,64,64]{2,1,0:T(8,128)S(1)}, f32[8,64]{1,0:T(8,128)S(1)}, bf16[8,512,1536]{2,1,0:T(8,128)(2,1)}, s32[8]{0:T(128)S(1)}, /*index...) while((s32[]{:T(128)}, f32[8,64,64]{2,1,0:T(8,128)S(1)}, ...), condition=%wide.region_21.22_spmd, body=%wide.region_20.21_spmd.sunk | while | flops 2815500288 | bytes 89005016 | solution.py:352
  1517.2 12.9 psum.77
  1546.3 38.9 %all-reduce.1 = (f32[512]{0:T(512)}, f32[512]{0:T(512)}, f32[512]{0:T(512)}, f32[512]{0:T(512)}, f32[512]{0:T(512)}) all-reduce(f32[512]{0:T(512)S(1)} %get-tuple-element.848, f32[512]{0:T(512)S(1)} %get-tuple-element.977, f32[512]{0:T(512)S(1)} %copy-done.48, f32[512]{0:T(512)S(1)} %copy-done.49, ...), channel_id=1, replica_groups=mesh['dp'=8,'mp'=4] {'dp','mp'}, use_global_device_ids=true, to_apply=%region_27.28 | all-reduce | flops 2560 | bytes 20480 | tf_op jit(solution)/shard_map/psum | solution.py:367
  1585.2 71.9 %all-reduce.7.cloned.1.call-done = (f32[512,1536]{1,0:T(8,128)}, f32[512,512]{1,0:T(8,128)}) async-done(((f32[512,1536]{1,0:T(8,128)}, f32[512,512]{1,0:T(8,128)}), (f32[512,1536]{1,0:T(8,128)}, f32[512,512]{1,0:T(8,128)})) %all-reduce.7.cloned.1.call-update) | async-done | bytes 4194320 | tf_op jit(solution)/shard_map/psum | solution.py:367
  (765 shorter events, 861.3 us)
Async XLA Ops:
  7.2 730.0 %copy-start = (bf16[512,512]{1,0:T(8,128)(2,1)S(1)}, bf16[512,512]{1,0:T(8,128)(2,1)}, u32[]{:S(2)}) copy-start(bf16[512,512]{1,0:T(8,128)(2,1)} %param.28) | copy-start | bytes 1572868
  7.2 8.6 copy-start.59
  7.2 88.1 %all-gather.9.cloned.1.call-start = ((), (), s32[]{:S(2)}) async-start(), calls=%async_computation.2 | async-start | bytes 5242880 | tf_op jit(solution)/shard_map/all_gather | solution.py:148
  8.8 93.1 %copy-start.7 = (bf16[1024,512]{0,1:T(8,128)(2,1)}, bf16[1024,512]{0,1:T(8,128)(2,1)S(1)}, u32[]{:S(2)}) copy-start(bf16[1024,512]{0,1:T(8,128)(2,1)S(1)} %copy.149) | copy-start | bytes 3145732
  11.8 725.5 %all-gather.11.cloned.1.call-start = ((), (), s32[]{:S(2)}) async-start(), calls=%async_computation.3 | async-start | bytes 5242880 | tf_op jit(solution)/shard_map/all_gather | solution.py:223
  15.2 86.6 %copy-start.28 = (f32[4096]{0:T(1024)}, f32[4096]{0:T(1024)S(1)}, u32[]{:S(2)}) copy-start(f32[4096]{0:T(1024)S(1)} %get-tuple-element.953) | copy-start | bytes 49156
  584.6 11.0 copy-start.45
  627.6 14.3 copy-start.26
  632.4 13.5 copy-start.29
  632.4 13.5 copy-start.31
  646.0 7.0 copy-start.8
  658.8 159.3 %all-gather.13.cloned.1.call-start = ((), (), s32[]{:S(2)}) async-start(), calls=%async_computation.5 | async-start | bytes 5242880 | tf_op jit(solution)/shard_map/all_gather | solution.py:232
  659.5 249.3 %reduce-scatter.5.cloned.1.call-start = ((), (), s32[]{:S(2)}) async-start(), calls=%async_computation.6 | async-start | bytes 5242880 | tf_op jit(solution)/shard_map/reduce_scatter | solution.py:242
  833.3 154.9 %reduce-scatter.3.cloned.1.call-start = ((), (), s32[]{:S(2)}) async-start(), calls=%async_computation.4 | async-start | bytes 5242880 | tf_op jit(solution)/shard_map/reduce_scatter | solution.py:226
  840.9 67.9 %copy-start.33 = (f32[1024]{0:T(1024)S(1)}, f32[1024]{0:T(1024)}, u32[]{:S(2)}) copy-start(f32[1024]{0:T(1024)} %copy-done.32) | copy-start | bytes 12292
  840.9 67.9 %copy-start.37 = (f32[1024]{0:T(1024)S(1)}, f32[1024]{0:T(1024)}, u32[]{:S(2)}) copy-start(f32[1024]{0:T(1024)} %copy-done.36) | copy-start | bytes 12292
  840.9 67.9 %copy-start.42 = (f32[512]{0:T(512)S(1)}, f32[512]{0:T(512)}, u32[]{:S(2)}) copy-start(f32[512]{0:T(512)} %param.26) | copy-start | bytes 6148
  840.9 147.3 %copy-start.51 = (f32[512]{0:T(512)S(1)}, f32[512]{0:T(512)}, u32[]{:S(2)}) copy-start(f32[512]{0:T(512)} %param.31) | copy-start | bytes 6148
  840.9 236.4 %all-gather.15.cloned.1.call-start = ((), (), s32[]{:S(2)}) async-start(), calls=%async_computation.7 | async-start | bytes 5242880 | tf_op jit(solution)/shard_map/all_gather | solution.py:264
  996.0 589.2 %all-reduce.9.cloned.1.call-start = ((), (), s32[]{:S(2)}) async-start(), calls=%async_computation.9 | async-start | bytes 4194304 | tf_op jit(solution)/shard_map/psum | solution.py:250
  1007.7 649.3 %all-reduce.7.cloned.1.call-start = ((), (), s32[]{:S(2)}) async-start(), calls=%async_computation.8 | async-start | bytes 8388608 | tf_op jit(solution)/shard_map/psum | solution.py:367
  1084.4 22.6 %copy-start.5 = (f32[4096,512]{0,1:T(8,128)S(1)}, f32[4096,512]{0,1:T(8,128)}, u32[]{:S(2)}) copy-start(f32[4096,512]{0,1:T(8,128)} %copy.158) | copy-start | bytes 25165828
  1109.8 14.7 copy-start.58
  1516.5 13.6 copy-start.20
  (73 other events, 242.4 us)
Sparse Core Ops, SparseCore 0:
  11.9 83.4 all-gather.8
  658.9 78.2 all-gather.10
  738.8 79.2 all-gather.12
  833.4 75.2 reduce-scatter.4
  910.9 77.2 reduce-scatter.2
  996.1 81.2 all-gather.14
  1080.7 61.3 all-reduce.8
  1516.7 140.3 all-reduce.6
where the time goes:
time: 1690 us; the launch traced here: 1670 us
  waiting for transfers between devices  468 us (28%)
  local copies, waits for them, and re-layouts  449 us (27%)
  matrix products  431 us (26%)
  other arithmetic  139 us (8%)
  blocking collectives  109 us (6%)
  loops' own time  48.6 us (3%)
    dynamic_update_slice x16, local copies, waits for them, and re-layouts, local(): lax.scan(forward_block, (zero_state, zero_total), jnp.arange(blocks, dtyp...  183 us
    reduce_scatter x1, waiting for transfers between devices, local(): lax.psum_scatter(jnp.dot(hidden_low, down_weight, preferred_element_type=...  76.8 us
    all_gather x1, waiting for transfers between devices, local(): group_second = lax.all_gather(second_low, 'mp', axis=0, tiled=True)  76.4 us
    psum x1, waiting for transfers between devices, local(): lax.psum((grad_qkv, grad_out, grad_gain_one, grad_shift_one, grad_gain_tw...  71.9 us
    all_gather x1, waiting for transfers between devices, local(): lax.all_gather(grad_context_own, 'mp', axis=0, tiled=True)  66.3 us
    all_gather x1, waiting for transfers between devices, local(): group_rows = lax.all_gather(normed_low, 'mp', axis=0, tiled=True)  62.3 us
    all_gather x1, waiting for transfers between devices, local(): group_cotangent = lax.all_gather(cotangent, 'mp', axis=0, tiled=True)  58 us
    reduce_scatter x1, waiting for transfers between devices, local(): lax.psum_scatter(jnp.einsum('tf,df->td', hidden_grad, up_weight, preferre...  55.1 us
  transfers between devices with their start and end apart: 8, of which 7 were waited for; matrix products, arithmetic and copies ran while one was open for 26% of the time, Pallas kernels for 0%

commit v1 on v0

--- a/solution.py
+++ b/solution.py
@@ -220,7 +220,14 @@
     normed_two, scaled_two, inv_two = normalize(residual, norm2_gain, norm2_shift)
     second_low = normed_two.astype(jnp.bfloat16)
     cotangent_wide = cotangent.astype(jnp.float32)
-    group_second = lax.all_gather(second_low, "mp", axis=0, tiled=True)
+    ways, here = (lax.axis_size("mp"), lax.axis_index("mp"))
+    group_second, reach = (second_low, 1)
+    while reach < ways:
+        theirs = lax.ppermute(group_second, "mp", [(d, d ^ reach) for d in range(ways)])
+        mine_first = jnp.concatenate([group_second, theirs], axis=0)
+        theirs_first = jnp.concatenate([theirs, group_second], axis=0)
+        group_second = jnp.where(here & reach == 0, mine_first, theirs_first)
+        reach = 2 * reach
     hidden_in = jnp.dot(group_second, up_weight, preferred_element_type=jnp.float32) + up_bias
     hidden_low = jax.nn.gelu(hidden_in, approximate=False).astype(jnp.bfloat16)
     ffn_out = lax.psum_scatter(

time: 1690 us -> 1750 us (1.036)
  waiting for transfers between devices: 468 us -> 529 us
    ppermute x0 -> x2, waiting for transfers between devices: none -> 184 us  [local(): lax.ppermute(group_second, 'mp', [(d, d ^ reach) for d in range(ways)])]
    all_gather x1 -> x0, waiting for transfers between devices: 76.4 us -> none  [local(): group_second = lax.all_gather(second_low, 'mp', axis=0, tiled=True)]
    all_gather x1, waiting for transfers between devices: 58 us -> 0.01 us  [local(): group_cotangent = lax.all_gather(cotangent, 'mp', axis=0, tiled=True)]
  transfers between devices with their start and end apart: 8 -> 9, of which waited for: 7 -> 7; matrix products, arithmetic and copies ran while one was open for 26% -> 26% of each run, Pallas kernels for 0% -> 0%
where the time goes in v1:
time: 1750 us; the launch traced here: 1730 us
  waiting for transfers between devices  529 us (30%)
  matrix products  438 us (25%)
  local copies, waits for them, and re-layouts  436 us (25%)
  other arithmetic  151 us (9%)
  blocking collectives  110 us (6%)
  loops' own time  48.8 us (3%)
    ppermute x2, waiting for transfers between devices, local(): lax.ppermute(group_second, 'mp', [(d, d ^ reach) for d in range(ways)])  184 us
    dynamic_update_slice x16, local copies, waits for them, and re-layouts, local(): lax.scan(forward_block, (zero_state, zero_total), jnp.arange(blocks, dtyp...  184 us
    psum x1, waiting for transfers between devices, local(): lax.psum((grad_qkv, grad_out, grad_gain_one, grad_shift_one, grad_gain_tw...  78.5 us
    reduce_scatter x1, waiting for transfers between devices, local(): lax.psum_scatter(jnp.dot(hidden_low, down_weight, preferred_element_type=...  76.5 us
    reduce_scatter x1, waiting for transfers between devices, local(): lax.psum_scatter(jnp.einsum('tf,df->td', hidden_grad, up_weight, preferre...  66.5 us
    all_gather x1, waiting for transfers between devices, local(): lax.all_gather(grad_context_own, 'mp', axis=0, tiled=True)  62.1 us
    all_gather x1, waiting for transfers between devices, local(): group_rows = lax.all_gather(normed_low, 'mp', axis=0, tiled=True)  61.3 us
    dot_general x8, matrix products, forward_block(): jnp.einsum('ihd,jhd->hij', query_low, key_low, preferred_element_type=jnp...  46.3 us
  transfers between devices with their start and end apart: 9, of which 7 were waited for; matrix products, arithmetic and copies ran while one was open for 26% of the time, Pallas kernels for 0%

profile of v1, /device:TPU:0, one launch (start us, length us, event | category | flops | bytes accessed | tf_op | source)
XLA Modules:
  0.0 1731.1 jit_solution(11487449149077086337)
XLA Ops:
  20.4 15.5 all-reduce
  36.0 61.3 %all-gather.8.cloned.1.call-done = bf16[4096,512]{1,0:T(8,128)(2,1)} async-done(((bf16[1024,512]{1,0:T(8,128)(2,1)}), bf16[4096,512]{1,0:T(8,128)(2,1)}) %all-gather.8.cloned.1.call-update) | async-done | bytes 4194320 | tf_op jit(solution)/shard_map/all_gather | solution.py:148
  97.4 483.3 %while.75 = (s32[]{:T(128)}, f32[8,64,64]{2,1,0:T(8,128)S(1)}, f32[8,64]{1,0:T(8,128)S(1)}, f32[8,512,8,64]{1,0,3,2:T(8,128)}, f32[8,512,8]{1,2,0:T(8,128)}, /*i...) while((s32[]{:T(128)}, f32[8,64,64]{2,1,0:T(8,128)S(1)}, ...), condition=%wide.region_8.9_spmd.clone, body=%wide.region_5.8_spmd.clone.sunk | while | flops 1599254528 | bytes 64349520 | solution.py:196
  128.5 21.9 %dynamic_update_slice.51 = f32[8,512,8,64]{1,0,3,2:T(8,128)} dynamic-update-slice(f32[8,512,8,64]{1,0,3,2:T(8,128)} %get-tuple-element.1103, f32[1,512,8,64]{1,0,3,2:T(1,128)S(1)} %copy.172, s32[]{:T(128)} %get-tuple-element.1100, s32[]{:T(128)} %constant.255.clone.1..sunk.2, s32[]{:T(128)} %constant.255.clone.1..sunk.2, s32[]{:T(128)} %constant.255.clone.1..sunk.2) | dynamic-update-slice | bytes 2097156 | tf_op jit(solution)/shard_map/while/body/jit(dynamic_update_index_in_dim)/dynamic_update_slice | solution.py:196
  189.0 21.9 %dynamic_update_slice.51 = f32[8,512,8,64]{1,0,3,2:T(8,128)} dynamic-update-slice(f32[8,512,8,64]{1,0,3,2:T(8,128)} %get-tuple-element.1103, f32[1,512,8,64]{1,0,3,2:T(1,128)S(1)} %copy.172, s32[]{:T(128)} %get-tuple-element.1100, s32[]{:T(128)} %constant.255.clone.1..sunk.2, s32[]{:T(128)} %constant.255.clone.1..sunk.2, s32[]{:T(128)} %constant.255.clone.1..sunk.2) | dynamic-update-slice | bytes 2097156 | tf_op jit(solution)/shard_map/while/body/jit(dynamic_update_index_in_dim)/dynamic_update_slice | solution.py:196
  249.4 21.9 %dynamic_update_slice.51 = f32[8,512,8,64]{1,0,3,2:T(8,128)} dynamic-update-slice(f32[8,512,8,64]{1,0,3,2:T(8,128)} %get-tuple-element.1103, f32[1,512,8,64]{1,0,3,2:T(1,128)S(1)} %copy.172, s32[]{:T(128)} %get-tuple-element.1100, s32[]{:T(128)} %constant.255.clone.1..sunk.2, s32[]{:T(128)} %constant.255.clone.1..sunk.2, s32[]{:T(128)} %constant.255.clone.1..sunk.2) | dynamic-update-slice | bytes 2097156 | tf_op jit(solution)/shard_map/while/body/jit(dynamic_update_index_in_dim)/dynamic_update_slice | solution.py:196
  309.8 21.9 %dynamic_update_slice.51 = f32[8,512,8,64]{1,0,3,2:T(8,128)} dynamic-update-slice(f32[8,512,8,64]{1,0,3,2:T(8,128)} %get-tuple-element.1103, f32[1,512,8,64]{1,0,3,2:T(1,128)S(1)} %copy.172, s32[]{:T(128)} %get-tuple-element.1100, s32[]{:T(128)} %constant.255.clone.1..sunk.2, s32[]{:T(128)} %constant.255.clone.1..sunk.2, s32[]{:T(128)} %constant.255.clone.1..sunk.2) | dynamic-update-slice | bytes 2097156 | tf_op jit(solution)/shard_map/while/body/jit(dynamic_update_index_in_dim)/dynamic_update_slice | solution.py:196
  370.2 21.9 %dynamic_update_slice.51 = f32[8,512,8,64]{1,0,3,2:T(8,128)} dynamic-update-slice(f32[8,512,8,64]{1,0,3,2:T(8,128)} %get-tuple-element.1103, f32[1,512,8,64]{1,0,3,2:T(1,128)S(1)} %copy.172, s32[]{:T(128)} %get-tuple-element.1100, s32[]{:T(128)} %constant.255.clone.1..sunk.2, s32[]{:T(128)} %constant.255.clone.1..sunk.2, s32[]{:T(128)} %constant.255.clone.1..sunk.2) | dynamic-update-slice | bytes 2097156 | tf_op jit(solution)/shard_map/while/body/jit(dynamic_update_index_in_dim)/dynamic_update_slice | solution.py:196
  430.6 21.9 %dynamic_update_slice.51 = f32[8,512,8,64]{1,0,3,2:T(8,128)} dynamic-update-slice(f32[8,512,8,64]{1,0,3,2:T(8,128)} %get-tuple-element.1103, f32[1,512,8,64]{1,0,3,2:T(1,128)S(1)} %copy.172, s32[]{:T(128)} %get-tuple-element.1100, s32[]{:T(128)} %constant.255.clone.1..sunk.2, s32[]{:T(128)} %constant.255.clone.1..sunk.2, s32[]{:T(128)} %constant.255.clone.1..sunk.2) | dynamic-update-slice | bytes 2097156 | tf_op jit(solution)/shard_map/while/body/jit(dynamic_update_index_in_dim)/dynamic_update_slice | solution.py:196
  491.0 21.9 %dynamic_update_slice.51 = f32[8,512,8,64]{1,0,3,2:T(8,128)} dynamic-update-slice(f32[8,512,8,64]{1,0,3,2:T(8,128)} %get-tuple-element.1103, f32[1,512,8,64]{1,0,3,2:T(1,128)S(1)} %copy.172, s32[]{:T(128)} %get-tuple-element.1100, s32[]{:T(128)} %constant.255.clone.1..sunk.2, s32[]{:T(128)} %constant.255.clone.1..sunk.2, s32[]{:T(128)} %constant.255.clone.1..sunk.2) | dynamic-update-slice | bytes 2097156 | tf_op jit(solution)/shard_map/while/body/jit(dynamic_update_index_in_dim)/dynamic_update_slice | solution.py:196
  551.4 21.9 %dynamic_update_slice.51 = f32[8,512,8,64]{1,0,3,2:T(8,128)} dynamic-update-slice(f32[8,512,8,64]{1,0,3,2:T(8,128)} %get-tuple-element.1103, f32[1,512,8,64]{1,0,3,2:T(1,128)S(1)} %copy.172, s32[]{:T(128)} %get-tuple-element.1100, s32[]{:T(128)} %constant.255.clone.1..sunk.2, s32[]{:T(128)} %constant.255.clone.1..sunk.2, s32[]{:T(128)} %constant.255.clone.1..sunk.2) | dynamic-update-slice | bytes 2097156 | tf_op jit(solution)/shard_map/while/body/jit(dynamic_update_index_in_dim)/dynamic_update_slice | solution.py:196
  580.8 10.9 all-gather
  600.8 22.8 %while.76 = (s32[]{:T(128)}, f32[8,64,64]{2,1,0:T(8,128)}, f32[8,64]{1,0:T(8,128)S(1)}, s32[]{:T(128)}, bf16[8,8,64,64]{3,2,1,0:T(8,128)(2,1)S(1)}, /*index=5*/b...) while((s32[]{:T(128)}, f32[8,64,64]{2,1,0:T(8,128)}, ...), condition=%wide.region_10.11_spmd.clone, body=%wide.region_9.10_spmd.clone.sunk | while | flops 166405 | bytes 332957 | solution.py:34
  652.5 25.7 %collective-permute-done = bf16[1024,512]{1,0:T(8,128)(2,1)} collective-permute-done((bf16[1024,512]{1,0:T(8,128)(2,1)}, bf16[1024,512]{1,0:T(8,128)(2,1)}, u32[]{:S(2)}, u32[]{:S(2)}) %collective-permute-start) | collective-permute-done | bytes 1048608 | tf_op jit(solution)/shard_map/ppermute | solution.py:226
  684.4 158.6 %collective-permute-done.1 = bf16[2048,512]{1,0:T(8,128)(2,1)} collective-permute-done((bf16[2048,512]{1,0:T(8,128)(2,1)}, bf16[2048,512]{1,0:T(8,128)(2,1)}, u32[]{:S(2)}, u32[]{:S(2)}) %collective-permute-start.1) | collective-permute-done | bytes 2097184 | tf_op jit(solution)/shard_map/ppermute | solution.py:226
  843.0 25.0 %fusion.89 = (bf16[4096,512]{1,0:T(8,128)(2,1)}, f32[4096,512]{1,0:T(8,128)}) fusion(f32[512]{0:T(512)S(1)} %convert_element_type.335, bf16[512,512]{1,0:T(8,128)(2,1)S(1)} %copy-done, bf16[2048,512]{1,0:T(8,128)(2,1)} %collective-permute-done.1, bf16[2048,512]{1,0:T(8,128)(2,1)} %maximum_select_fusion.1, pred[]{:T(512)S(6)} %eq.158), kind=kOutput, calls=%fused_computation.135 | convolution fusion | flops 2304770048 | bytes 17303552 | tf_op jit(solution)/shard_map/dot_general | solution.py:231
  891.2 66.5 %reduce-scatter.5.cloned.1.call-done = bf16[1024,512]{1,0:T(8,128)(2,1)} async-done(((bf16[4096,512]{1,0:T(8,128)(2,1)}), bf16[1024,512]{1,0:T(8,128)(2,1)}) %reduce-scatter.5.cloned.1.call-update) | async-done | bytes 1048592 | tf_op jit(solution)/shard_map/reduce_scatter | solution.py:249
  960.6 76.5 %reduce-scatter.3.cloned.1.call-done = bf16[1024,512]{1,0:T(8,128)(2,1)} async-done(((bf16[4096,512]{1,0:T(8,128)(2,1)}), bf16[1024,512]{1,0:T(8,128)(2,1)}) %reduce-scatter.3.cloned.1.call-update) | async-done | bytes 1048592 | tf_op jit(solution)/shard_map/reduce_scatter | solution.py:233
  1063.5 62.1 %all-gather.12.cloned.1.call-done = bf16[4096,512]{1,0:T(8,128)(2,1)} async-done(((bf16[1024,512]{1,0:T(8,128)(2,1)}), bf16[4096,512]{1,0:T(8,128)(2,1)}) %all-gather.12.cloned.1.call-update) | async-done | bytes 4194320 | tf_op jit(solution)/shard_map/all_gather | solution.py:271
  1159.4 13.1 all-gather.2
  1188.1 382.5 %while.74 = (s32[]{:T(128)}, f32[8,64,64]{2,1,0:T(8,128)S(1)}, f32[8,64]{1,0:T(8,128)S(1)}, bf16[8,512,1536]{2,1,0:T(8,128)(2,1)}, s32[8]{0:T(128)S(1)}, /*index...) while((s32[]{:T(128)}, f32[8,64,64]{2,1,0:T(8,128)S(1)}, ...), condition=%wide.region_21.22_spmd, body=%wide.region_20.21_spmd.sunk | while | flops 2815500288 | bytes 89005016 | solution.py:359
  1576.9 12.6 psum.77
  1595.8 39.5 %all-reduce.1 = (f32[512]{0:T(512)}, f32[512]{0:T(512)}, f32[512]{0:T(512)}, f32[512]{0:T(512)}, f32[512]{0:T(512)}) all-reduce(f32[512]{0:T(512)S(1)} %get-tuple-element.658, f32[512]{0:T(512)S(1)} %get-tuple-element.661, f32[512]{0:T(512)S(1)} %copy-done.37, f32[512]{0:T(512)S(1)} %copy-done.38, ...), channel_id=1, replica_groups=mesh['dp'=8,'mp'=4] {'dp','mp'}, use_global_device_ids=true, to_apply=%region_27.28 | all-reduce | flops 2560 | bytes 20480 | tf_op jit(solution)/shard_map/psum | solution.py:374
  1638.5 78.5 %all-reduce.7.cloned.1.call-done = (f32[512,1536]{1,0:T(8,128)}, f32[512,512]{1,0:T(8,128)}) async-done(((f32[512,1536]{1,0:T(8,128)}, f32[512,512]{1,0:T(8,128)}), (f32[512,1536]{1,0:T(8,128)}, f32[512,512]{1,0:T(8,128)})) %all-reduce.7.cloned.1.call-update) | async-done | bytes 4194320 | tf_op jit(solution)/shard_map/psum | solution.py:374
  (738 shorter events, 855.6 us)
Async XLA Ops:
  7.2 835.8 %copy-start = (bf16[512,512]{1,0:T(8,128)(2,1)S(1)}, bf16[512,512]{1,0:T(8,128)(2,1)}, u32[]{:S(2)}) copy-start(bf16[512,512]{1,0:T(8,128)(2,1)} %param.28) | copy-start | bytes 1572868
  7.2 11.2 copy-start.47
  7.2 90.2 %all-gather.8.cloned.1.call-start = ((), (), s32[]{:S(2)}) async-start(), calls=%async_computation.2 | async-start | bytes 5242880 | tf_op jit(solution)/shard_map/all_gather | solution.py:148
  13.8 854.3 %all-gather.10.cloned.1.call-start = ((), (), s32[]{:S(2)}) async-start(), calls=%async_computation.4 | async-start | bytes 5242880 | tf_op jit(solution)/shard_map/all_gather | solution.py:239
  580.7 11.0 copy-start.33
  580.7 47.6 %copy-start.22 = (s32[4096]{0:T(1024)}, s32[4096]{0:T(1024)S(1)}, u32[]{:S(2)}) copy-start(s32[4096]{0:T(1024)S(1)} %get-tuple-element.1315) | copy-start | bytes 49156
  628.4 13.5 copy-start.24
  628.4 13.5 copy-start.26
  652.5 25.7 %collective-permute-start = (bf16[1024,512]{1,0:T(8,128)(2,1)}, bf16[1024,512]{1,0:T(8,128)(2,1)}, u32[]{:S(2)}, u32[]{:S(2)}) collective-permute-start(bf16[1024,512]{1,0:T(8,128)(2,1)} %add_convert_fusion.2), channel_id=1, source_target_pairs={{0,1},{1,0},{2,3},{3,2},{4,5},{5,4},{6,7},{7,6},{8,9},{9,8},{10,11... | collective-permute-start | bytes 3145736 | tf_op jit(solution)/shard_map/ppermute | solution.py:226
  682.4 160.6 %collective-permute-start.1 = (bf16[2048,512]{1,0:T(8,128)(2,1)}, bf16[2048,512]{1,0:T(8,128)(2,1)}, u32[]{:S(2)}, u32[]{:S(2)}) collective-permute-start(bf16[2048,512]{1,0:T(8,128)(2,1)} %maximum_select_fusion.1), channel_id=1, source_target_pairs={{0,2},{1,3},{2,0},{3,1},{4,6},{5,7},{6,4},{7,5},{8,10},{9,11},{10,... | collective-permute-start | bytes 6291464 | tf_op jit(solution)/shard_map/ppermute | solution.py:226
  683.3 274.4 %reduce-scatter.5.cloned.1.call-start = ((), (), s32[]{:S(2)}) async-start(), calls=%async_computation.5 | async-start | bytes 5242880 | tf_op jit(solution)/shard_map/reduce_scatter | solution.py:249
  684.4 158.6 %copy-start.41 = (f32[512]{0:T(512)}, f32[512]{0:T(512)S(1)}, u32[]{:S(2)}) copy-start(f32[512]{0:T(512)S(1)} %convert_element_type.335) | copy-start | bytes 6148
  883.3 153.9 %reduce-scatter.3.cloned.1.call-start = ((), (), s32[]{:S(2)}) async-start(), calls=%async_computation.3 | async-start | bytes 5242880 | tf_op jit(solution)/shard_map/reduce_scatter | solution.py:233
  890.9 146.2 %copy-start.40 = (f32[512]{0:T(512)S(1)}, f32[512]{0:T(512)}, u32[]{:S(2)}) copy-start(f32[512]{0:T(512)} %param.31) | copy-start | bytes 6148
  890.9 234.7 %all-gather.12.cloned.1.call-start = ((), (), s32[]{:S(2)}) async-start(), calls=%async_computation.6 | async-start | bytes 5242880 | tf_op jit(solution)/shard_map/all_gather | solution.py:271
  1044.3 594.2 %all-reduce.9.cloned.1.call-start = ((), (), s32[]{:S(2)}) async-start(), calls=%async_computation.8 | async-start | bytes 4194304 | tf_op jit(solution)/shard_map/psum | solution.py:257
  1052.8 7.5 copy-start.8
  1060.2 656.8 %all-reduce.7.cloned.1.call-start = ((), (), s32[]{:S(2)}) async-start(), calls=%async_computation.7 | async-start | bytes 8388608 | tf_op jit(solution)/shard_map/psum | solution.py:374
  1132.7 22.5 %copy-start.5 = (f32[4096,512]{0,1:T(8,128)S(1)}, f32[4096,512]{0,1:T(8,128)}, u32[]{:S(2)}) copy-start(f32[4096,512]{0,1:T(8,128)} %copy.113) | copy-start | bytes 25165828
  1158.1 14.4 copy-start.46
  1576.2 13.2 copy-start.28
  1576.2 13.2 copy-start.30
  1576.2 13.2 copy-start.36
  1589.5 45.8 %copy-start.9 = (f32[1024,512]{1,0:T(8,128)S(1)}, f32[1024,512]{1,0:T(8,128)}, u32[]{:S(2)}) copy-start(f32[1024,512]{1,0:T(8,128)} %copy-done.7) | copy-start | bytes 6291460
  (63 other events, 219.8 us)
Sparse Core Ops, SparseCore 0:
  13.9 83.4 all-gather.7
  683.4 148.6 all-gather.9
  883.4 74.2 reduce-scatter.4
  959.8 77.2 reduce-scatter.2
  1044.4 81.2 all-gather.11
  1128.8 61.3 all-reduce.8
  1576.4 140.5 all-reduce.6
